TPU v7x, 512 devices: a whole 4x4x16 slice. The times are simulated.
512 devices in a mesh: tm: 64 (over y, z), state: 8 (over x, core).
Axes of the slice: x: 4, y: 4, z: 16, core: 2. Of those that a mesh axis runs over, the one named last changes fastest.
Arguments:
- obs: int32 [512], P('tm'), may hold values from 0 to 255
- emit_logits: float32 [256, 2048], P(None, 'state'), may hold values from -0.6 to 0.6
- trans_logits: float32 [16, 3, 128, 128], P('state'), may hold values from -5 to 17
- band_cols: int32 [16, 3], replicated, may hold values from 0 to 15, as said below
- init_logits: float32 [2048], replicated, may hold values from -6 to 6
Outputs:
- posterior: float32 [64, 2048], P('tm', 'state')
Inputs may be any that keep to these rules, and one draw needn't show every extreme that they name: Row r of band_cols names 3 different block columns, the first of them r itself.
All inputs are finite; a program needn't handle non-finite values.
Results may differ from a plain program's by a relative error of at most 0.0006.
The roundings to bfloat16 on the way count: a program that leaves them out, or rounds other values in their place, can miss the bound.
Values may be sent and summed in bfloat16 or wider, within the bound.
A program may use at most 64 MiB of HBM per device.

v0:
```python
import jax
import jax.numpy as jnp
from jax import lax
from jax.sharding import PartitionSpec as P

SEQS = 1
SMOOTH = 0.001


def from_behind(value, axis, steps):
    count = lax.axis_size(axis)
    initial, last = (max(0, -steps), min(count, count - steps))
    return lax.ppermute(value, axis, [(source, source + steps) for source in range(initial, last)])


def form_columns(emit_full, blocks, band_cols, first_col, col_count):
    states = emit_full.shape[1]
    block_count = blocks.shape[0]
    block_size = blocks.shape[2]
    state_rows = jnp.arange(states)[:, None]
    state_cols = first_col + jnp.arange(col_count)[None, :]
    matrix = (state_rows == state_cols).astype(jnp.float32)
    col_scale = jnp.zeros((col_count,), jnp.float32)
    for moment in range(emit_full.shape[0] - 1, -1, -1):
        scaled = (jnp.exp(emit_full[moment])[:, None] * matrix).astype(jnp.bfloat16)
        picked = scaled.reshape(block_count, block_size, col_count)[band_cols]
        product = jnp.einsum(
            "rkij,rkjc->ric", blocks, picked, preferred_element_type=jnp.float32
        ).reshape(states, col_count)
        matrix = product + SMOOTH / states * jnp.sum(scaled, axis=0, dtype=jnp.float32)[None, :]
        col_peak = jnp.max(matrix, axis=0)
        matrix = matrix / col_peak[None, :]
        col_scale = col_scale + jnp.log(col_peak)
    return jnp.log(matrix) + col_scale[None, :]


def on_device(obs, emit_logits, trans_logits, band_cols, init_logits):
    col_count = emit_logits.shape[1]
    state_index = lax.axis_index("state")
    first_col = state_index * col_count
    groups = lax.axis_size("tm") // SEQS
    position = lax.axis_index("tm") % groups
    blocks_own = ((1.0 - SMOOTH) * jax.nn.softmax(trans_logits, axis=(1, 3))).astype(jnp.bfloat16)
    blocks = lax.all_gather(blocks_own, "state", axis=0, tiled=True)
    log_emit = jax.nn.log_softmax(emit_logits, axis=0)
    symbols = emit_logits.shape[0]
    onehot = (obs[:, None] == jnp.arange(symbols)[None, :]).astype(jnp.float32)
    emit_own = jnp.dot(onehot, log_emit, precision=lax.Precision.HIGHEST)
    emit_full = lax.all_gather(emit_own, "state", axis=1, tiled=True)
    own_log = form_columns(emit_full, blocks, band_cols, first_col, col_count)
    left_log = from_behind(own_log, "tm", 1)
    row_peak = lax.pmax(jnp.max(own_log, axis=1), "state")
    peak_own = lax.dynamic_slice_in_dim(row_peak, first_col, col_count)
    shifted = left_log + peak_own[None, :]
    left_peak = lax.pmax(jnp.max(shifted, axis=1), "state")
    weights = jnp.exp(shifted - left_peak[:, None]).astype(jnp.bfloat16)
    right_exp = jnp.exp(own_log - row_peak[:, None]).astype(jnp.bfloat16)
    prior_log = jax.nn.log_softmax(init_logits)
    summed = jnp.dot(
        lax.all_gather(weights, "state", axis=1, tiled=True),
        right_exp,
        preferred_element_type=jnp.float32,
    )
    pair_log = left_peak[:, None] + jnp.log(summed)
    chosen = jnp.where(position == 0, own_log, pair_log)
    col_max = jnp.max(chosen, axis=0)
    scaled_exp = jnp.exp(chosen - col_max[None, :])

    def apply_cols(vector):
        vector_top = jnp.max(vector)
        mixture = jnp.dot(
            jnp.exp(vector - vector_top)[None, :], scaled_exp, precision=lax.Precision.HIGHEST
        )[0]
        return vector_top + col_max + jnp.log(mixture)

    start_cols = apply_cols(prior_log)

    def advance(counter, current):
        incoming = from_behind(current, "tm", 2)
        whole_vector = lax.all_gather(incoming, "state", axis=0, tiled=True)
        return jnp.where(position < 2, start_cols, apply_cols(whole_vector))

    alpha_cols = lax.fori_loop(0, groups // 2 - 1, advance, start_cols)
    vector_top = lax.pmax(jnp.max(alpha_cols), "state")
    total_sum = lax.psum(jnp.sum(jnp.exp(alpha_cols - vector_top)), "state")
    posterior = alpha_cols - vector_top - jnp.log(total_sum)
    return posterior[None, :]


def solution(mesh):
    return jax.shard_map(
        on_device,
        mesh=mesh,
        in_specs=(P("tm"), P(None, "state"), P("state", None, None, None), P(), P()),
        out_specs=P("tm", "state"),
        check_vma=False,
    )
```

profile of v0, /device:TPU:9, one launch (start us, length us, event | category | flops | bytes accessed | tf_op | source)
XLA Modules:
  0.0 896.2 jit_solution(222817929016838769)
XLA Ops:
  13.3 13.6 %all_gather.15 = f32[8,2048]{1,0:T(8,128)S(1)} all-gather(f32[8,256]{1,0:T(8,128)S(1)} %fusion.15), channel_id=1, replica_groups=mesh['tm'=64,'state'=8] {'state'}, dimensions={1}, use_global_device_ids=true | all-gather | bytes 73728 | tf_op jit(solution)/shard_map/all_gather | solution.py:49
  30.6 17.3 %all-gather.6.cloned.1.call-done = bf16[16,3,128,128]{3,2,1,0:T(8,128)(2,1)} async-done(((bf16[2,3,128,128]{3,2,1,0:T(8,128)(2,1)}), bf16[16,3,128,128]{3,2,1,0:T(8,128)(2,1)}) %all-gather.6.cloned.1.call-update) | async-done | bytes 1572880 | tf_op jit(solution)/shard_map/all_gather | solution.py:44
  98.6 12.8 %pmax.21 = f32[2048]{0:T(1024)S(1)} all-reduce(f32[2048]{0:T(1024)S(1)} %bitcast.156), channel_id=1, replica_groups=mesh['tm'=64,'state'=8] {'state'}, use_global_device_ids=true, to_apply=%region_24.25 | all-reduce | flops 2048 | bytes 16384 | tf_op jit(solution)/shard_map/pmax | solution.py:52
  111.5 33.2 %collective-permute-done.1 = f32[2048,256]{1,0:T(8,128)S(1)} collective-permute-done((f32[2048,256]{1,0:T(8,128)}, f32[2048,256]{1,0:T(8,128)S(1)}, u32[]{:S(2)}, u32[]{:S(2)}) %collective-permute-start.1) | collective-permute-done | bytes 2097184 | tf_op jit(solution)/shard_map/ppermute | solution.py:13
  145.1 12.8 %pmax.22 = f32[2048]{0:T(1024)S(1)} all-reduce(f32[2048]{0:T(1024)S(1)} %add_reduce_fusion.1), channel_id=1, replica_groups=mesh['tm'=64,'state'=8] {'state'}, use_global_device_ids=true, to_apply=%region_26.27 | all-reduce | flops 2048 | bytes 16384 | tf_op jit(solution)/shard_map/pmax | solution.py:55
  164.6 54.8 %all-gather.8.cloned.1.call-done = bf16[2048,2048]{1,0:T(8,128)(2,1)} async-done(((bf16[2048,256]{1,0:T(8,128)(2,1)}), bf16[2048,2048]{1,0:T(8,128)(2,1)}) %all-gather.8.cloned.1.call-update) | async-done | bytes 8388624 | tf_op jit(solution)/shard_map/all_gather | solution.py:60
  219.4 7.5 fusion.21
  228.7 630.8 %while.12 = (s32[]{:T(128)}, f32[256]{0:T(256)S(1)}, pred[]{:T(512)}, f32[256]{0:T(256)S(1)}, f32[2048,256]{1,0:T(8,128)S(1)}, /*index=5*/f32[256]{0:T(256)S(1)}, s32[]{:T(128)}, f32[]{:T(128)}) while((s32[]{:T(128)}, f32[256]{0:T(256)S(1)}, pred[]{:T(512)}, f32[256]{0:T(256)S(1)}, f32[2048,256]{1,0:T(8,128)S(1)}, ...), condition=%wide.region_30.31_spmd, body=%wide.region_28.30_spmd.sunk | while | flops 6296321 | bytes 2148494 | solution.py:83
  236.1 11.0 %all-gather.2 = f32[8,1,256]{2,1,0:T(1,128)S(1)} all-gather(f32[1,1,256]{2,1,0:T(1,128)S(1)} %bitcast.157), channel_id=1, replica_groups=mesh['tm'=64,'state'=8] {'state'}, dimensions={0}, use_global_device_ids=true | all-gather | bytes 9216 | tf_op jit(solution)/shard_map/while/body/eval_jaxpr/all_gather | solution.py:80
  257.5 9.0 %all-gather.2 = f32[8,1,256]{2,1,0:T(1,128)S(1)} all-gather(f32[1,1,256]{2,1,0:T(1,128)S(1)} %bitcast.157), channel_id=1, replica_groups=mesh['tm'=64,'state'=8] {'state'}, dimensions={0}, use_global_device_ids=true | all-gather | bytes 9216 | tf_op jit(solution)/shard_map/while/body/eval_jaxpr/all_gather | solution.py:80
  271.4 5.4 collective-permute-done
  276.8 10.9 %all-gather.2 = f32[8,1,256]{2,1,0:T(1,128)S(1)} all-gather(f32[1,1,256]{2,1,0:T(1,128)S(1)} %bitcast.157), channel_id=1, replica_groups=mesh['tm'=64,'state'=8] {'state'}, dimensions={0}, use_global_device_ids=true | all-gather | bytes 9216 | tf_op jit(solution)/shard_map/while/body/eval_jaxpr/all_gather | solution.py:80
  292.7 5.4 collective-permute-done
  298.1 9.0 %all-gather.2 = f32[8,1,256]{2,1,0:T(1,128)S(1)} all-gather(f32[1,1,256]{2,1,0:T(1,128)S(1)} %bitcast.157), channel_id=1, replica_groups=mesh['tm'=64,'state'=8] {'state'}, dimensions={0}, use_global_device_ids=true | all-gather | bytes 9216 | tf_op jit(solution)/shard_map/while/body/eval_jaxpr/all_gather | solution.py:80
  312.1 5.4 collective-permute-done
  317.4 10.9 %all-gather.2 = f32[8,1,256]{2,1,0:T(1,128)S(1)} all-gather(f32[1,1,256]{2,1,0:T(1,128)S(1)} %bitcast.157), channel_id=1, replica_groups=mesh['tm'=64,'state'=8] {'state'}, dimensions={0}, use_global_device_ids=true | all-gather | bytes 9216 | tf_op jit(solution)/shard_map/while/body/eval_jaxpr/all_gather | solution.py:80
  333.3 5.4 collective-permute-done
  338.7 9.0 %all-gather.2 = f32[8,1,256]{2,1,0:T(1,128)S(1)} all-gather(f32[1,1,256]{2,1,0:T(1,128)S(1)} %bitcast.157), channel_id=1, replica_groups=mesh['tm'=64,'state'=8] {'state'}, dimensions={0}, use_global_device_ids=true | all-gather | bytes 9216 | tf_op jit(solution)/shard_map/while/body/eval_jaxpr/all_gather | solution.py:80
  352.7 5.4 collective-permute-done
  358.1 10.9 %all-gather.2 = f32[8,1,256]{2,1,0:T(1,128)S(1)} all-gather(f32[1,1,256]{2,1,0:T(1,128)S(1)} %bitcast.157), channel_id=1, replica_groups=mesh['tm'=64,'state'=8] {'state'}, dimensions={0}, use_global_device_ids=true | all-gather | bytes 9216 | tf_op jit(solution)/shard_map/while/body/eval_jaxpr/all_gather | solution.py:80
  374.0 5.4 collective-permute-done
  379.4 9.0 %all-gather.2 = f32[8,1,256]{2,1,0:T(1,128)S(1)} all-gather(f32[1,1,256]{2,1,0:T(1,128)S(1)} %bitcast.157), channel_id=1, replica_groups=mesh['tm'=64,'state'=8] {'state'}, dimensions={0}, use_global_device_ids=true | all-gather | bytes 9216 | tf_op jit(solution)/shard_map/while/body/eval_jaxpr/all_gather | solution.py:80
  393.3 5.4 collective-permute-done
  398.7 10.9 %all-gather.2 = f32[8,1,256]{2,1,0:T(1,128)S(1)} all-gather(f32[1,1,256]{2,1,0:T(1,128)S(1)} %bitcast.157), channel_id=1, replica_groups=mesh['tm'=64,'state'=8] {'state'}, dimensions={0}, use_global_device_ids=true | all-gather | bytes 9216 | tf_op jit(solution)/shard_map/while/body/eval_jaxpr/all_gather | solution.py:80
  414.6 5.4 collective-permute-done
  420.0 9.0 %all-gather.2 = f32[8,1,256]{2,1,0:T(1,128)S(1)} all-gather(f32[1,1,256]{2,1,0:T(1,128)S(1)} %bitcast.157), channel_id=1, replica_groups=mesh['tm'=64,'state'=8] {'state'}, dimensions={0}, use_global_device_ids=true | all-gather | bytes 9216 | tf_op jit(solution)/shard_map/while/body/eval_jaxpr/all_gather | solution.py:80
  433.9 5.4 collective-permute-done
  439.3 10.9 %all-gather.2 = f32[8,1,256]{2,1,0:T(1,128)S(1)} all-gather(f32[1,1,256]{2,1,0:T(1,128)S(1)} %bitcast.157), channel_id=1, replica_groups=mesh['tm'=64,'state'=8] {'state'}, dimensions={0}, use_global_device_ids=true | all-gather | bytes 9216 | tf_op jit(solution)/shard_map/while/body/eval_jaxpr/all_gather | solution.py:80
  460.6 9.0 %all-gather.2 = f32[8,1,256]{2,1,0:T(1,128)S(1)} all-gather(f32[1,1,256]{2,1,0:T(1,128)S(1)} %bitcast.157), channel_id=1, replica_groups=mesh['tm'=64,'state'=8] {'state'}, dimensions={0}, use_global_device_ids=true | all-gather | bytes 9216 | tf_op jit(solution)/shard_map/while/body/eval_jaxpr/all_gather | solution.py:80
  479.9 10.9 %all-gather.2 = f32[8,1,256]{2,1,0:T(1,128)S(1)} all-gather(f32[1,1,256]{2,1,0:T(1,128)S(1)} %bitcast.157), channel_id=1, replica_groups=mesh['tm'=64,'state'=8] {'state'}, dimensions={0}, use_global_device_ids=true | all-gather | bytes 9216 | tf_op jit(solution)/shard_map/while/body/eval_jaxpr/all_gather | solution.py:80
  495.8 5.4 collective-permute-done
  501.2 9.0 %all-gather.2 = f32[8,1,256]{2,1,0:T(1,128)S(1)} all-gather(f32[1,1,256]{2,1,0:T(1,128)S(1)} %bitcast.157), channel_id=1, replica_groups=mesh['tm'=64,'state'=8] {'state'}, dimensions={0}, use_global_device_ids=true | all-gather | bytes 9216 | tf_op jit(solution)/shard_map/while/body/eval_jaxpr/all_gather | solution.py:80
  515.2 5.4 collective-permute-done
  520.6 10.9 %all-gather.2 = f32[8,1,256]{2,1,0:T(1,128)S(1)} all-gather(f32[1,1,256]{2,1,0:T(1,128)S(1)} %bitcast.157), channel_id=1, replica_groups=mesh['tm'=64,'state'=8] {'state'}, dimensions={0}, use_global_device_ids=true | all-gather | bytes 9216 | tf_op jit(solution)/shard_map/while/body/eval_jaxpr/all_gather | solution.py:80
  536.5 5.4 collective-permute-done
  541.9 9.0 %all-gather.2 = f32[8,1,256]{2,1,0:T(1,128)S(1)} all-gather(f32[1,1,256]{2,1,0:T(1,128)S(1)} %bitcast.157), channel_id=1, replica_groups=mesh['tm'=64,'state'=8] {'state'}, dimensions={0}, use_global_device_ids=true | all-gather | bytes 9216 | tf_op jit(solution)/shard_map/while/body/eval_jaxpr/all_gather | solution.py:80
  555.8 5.4 collective-permute-done
  561.2 10.9 %all-gather.2 = f32[8,1,256]{2,1,0:T(1,128)S(1)} all-gather(f32[1,1,256]{2,1,0:T(1,128)S(1)} %bitcast.157), channel_id=1, replica_groups=mesh['tm'=64,'state'=8] {'state'}, dimensions={0}, use_global_device_ids=true | all-gather | bytes 9216 | tf_op jit(solution)/shard_map/while/body/eval_jaxpr/all_gather | solution.py:80
  577.1 5.4 collective-permute-done
  582.5 9.0 %all-gather.2 = f32[8,1,256]{2,1,0:T(1,128)S(1)} all-gather(f32[1,1,256]{2,1,0:T(1,128)S(1)} %bitcast.157), channel_id=1, replica_groups=mesh['tm'=64,'state'=8] {'state'}, dimensions={0}, use_global_device_ids=true | all-gather | bytes 9216 | tf_op jit(solution)/shard_map/while/body/eval_jaxpr/all_gather | solution.py:80
  596.4 5.4 collective-permute-done
  601.8 10.9 %all-gather.2 = f32[8,1,256]{2,1,0:T(1,128)S(1)} all-gather(f32[1,1,256]{2,1,0:T(1,128)S(1)} %bitcast.157), channel_id=1, replica_groups=mesh['tm'=64,'state'=8] {'state'}, dimensions={0}, use_global_device_ids=true | all-gather | bytes 9216 | tf_op jit(solution)/shard_map/while/body/eval_jaxpr/all_gather | solution.py:80
  617.7 5.4 collective-permute-done
  623.1 9.0 %all-gather.2 = f32[8,1,256]{2,1,0:T(1,128)S(1)} all-gather(f32[1,1,256]{2,1,0:T(1,128)S(1)} %bitcast.157), channel_id=1, replica_groups=mesh['tm'=64,'state'=8] {'state'}, dimensions={0}, use_global_device_ids=true | all-gather | bytes 9216 | tf_op jit(solution)/shard_map/while/body/eval_jaxpr/all_gather | solution.py:80
  637.0 5.4 collective-permute-done
  642.4 10.9 %all-gather.2 = f32[8,1,256]{2,1,0:T(1,128)S(1)} all-gather(f32[1,1,256]{2,1,0:T(1,128)S(1)} %bitcast.157), channel_id=1, replica_groups=mesh['tm'=64,'state'=8] {'state'}, dimensions={0}, use_global_device_ids=true | all-gather | bytes 9216 | tf_op jit(solution)/shard_map/while/body/eval_jaxpr/all_gather | solution.py:80
  658.3 5.4 collective-permute-done
  663.7 9.0 %all-gather.2 = f32[8,1,256]{2,1,0:T(1,128)S(1)} all-gather(f32[1,1,256]{2,1,0:T(1,128)S(1)} %bitcast.157), channel_id=1, replica_groups=mesh['tm'=64,'state'=8] {'state'}, dimensions={0}, use_global_device_ids=true | all-gather | bytes 9216 | tf_op jit(solution)/shard_map/while/body/eval_jaxpr/all_gather | solution.py:80
  677.7 5.4 collective-permute-done
  683.1 10.9 %all-gather.2 = f32[8,1,256]{2,1,0:T(1,128)S(1)} all-gather(f32[1,1,256]{2,1,0:T(1,128)S(1)} %bitcast.157), channel_id=1, replica_groups=mesh['tm'=64,'state'=8] {'state'}, dimensions={0}, use_global_device_ids=true | all-gather | bytes 9216 | tf_op jit(solution)/shard_map/while/body/eval_jaxpr/all_gather | solution.py:80
  704.4 9.0 %all-gather.2 = f32[8,1,256]{2,1,0:T(1,128)S(1)} all-gather(f32[1,1,256]{2,1,0:T(1,128)S(1)} %bitcast.157), channel_id=1, replica_groups=mesh['tm'=64,'state'=8] {'state'}, dimensions={0}, use_global_device_ids=true | all-gather | bytes 9216 | tf_op jit(solution)/shard_map/while/body/eval_jaxpr/all_gather | solution.py:80
  723.7 10.9 %all-gather.2 = f32[8,1,256]{2,1,0:T(1,128)S(1)} all-gather(f32[1,1,256]{2,1,0:T(1,128)S(1)} %bitcast.157), channel_id=1, replica_groups=mesh['tm'=64,'state'=8] {'state'}, dimensions={0}, use_global_device_ids=true | all-gather | bytes 9216 | tf_op jit(solution)/shard_map/while/body/eval_jaxpr/all_gather | solution.py:80
  739.6 5.4 collective-permute-done
  745.0 9.0 %all-gather.2 = f32[8,1,256]{2,1,0:T(1,128)S(1)} all-gather(f32[1,1,256]{2,1,0:T(1,128)S(1)} %bitcast.157), channel_id=1, replica_groups=mesh['tm'=64,'state'=8] {'state'}, dimensions={0}, use_global_device_ids=true | all-gather | bytes 9216 | tf_op jit(solution)/shard_map/while/body/eval_jaxpr/all_gather | solution.py:80
  758.9 5.4 collective-permute-done
  764.3 10.9 %all-gather.2 = f32[8,1,256]{2,1,0:T(1,128)S(1)} all-gather(f32[1,1,256]{2,1,0:T(1,128)S(1)} %bitcast.157), channel_id=1, replica_groups=mesh['tm'=64,'state'=8] {'state'}, dimensions={0}, use_global_device_ids=true | all-gather | bytes 9216 | tf_op jit(solution)/shard_map/while/body/eval_jaxpr/all_gather | solution.py:80
  780.2 5.4 collective-permute-done
  785.6 9.0 %all-gather.2 = f32[8,1,256]{2,1,0:T(1,128)S(1)} all-gather(f32[1,1,256]{2,1,0:T(1,128)S(1)} %bitcast.157), channel_id=1, replica_groups=mesh['tm'=64,'state'=8] {'state'}, dimensions={0}, use_global_device_ids=true | all-gather | bytes 9216 | tf_op jit(solution)/shard_map/while/body/eval_jaxpr/all_gather | solution.py:80
  799.5 5.4 collective-permute-done
  804.9 10.9 %all-gather.2 = f32[8,1,256]{2,1,0:T(1,128)S(1)} all-gather(f32[1,1,256]{2,1,0:T(1,128)S(1)} %bitcast.157), channel_id=1, replica_groups=mesh['tm'=64,'state'=8] {'state'}, dimensions={0}, use_global_device_ids=true | all-gather | bytes 9216 | tf_op jit(solution)/shard_map/while/body/eval_jaxpr/all_gather | solution.py:80
  826.2 9.0 %all-gather.2 = f32[8,1,256]{2,1,0:T(1,128)S(1)} all-gather(f32[1,1,256]{2,1,0:T(1,128)S(1)} %bitcast.157), channel_id=1, replica_groups=mesh['tm'=64,'state'=8] {'state'}, dimensions={0}, use_global_device_ids=true | all-gather | bytes 9216 | tf_op jit(solution)/shard_map/while/body/eval_jaxpr/all_gather | solution.py:80
  845.6 10.9 %all-gather.2 = f32[8,1,256]{2,1,0:T(1,128)S(1)} all-gather(f32[1,1,256]{2,1,0:T(1,128)S(1)} %bitcast.157), channel_id=1, replica_groups=mesh['tm'=64,'state'=8] {'state'}, dimensions={0}, use_global_device_ids=true | all-gather | bytes 9216 | tf_op jit(solution)/shard_map/while/body/eval_jaxpr/all_gather | solution.py:80
  860.1 12.7 %pmax.23 = f32[]{:T(128)} all-reduce(f32[]{:T(128)} %reduce_max.175), channel_id=1, replica_groups=mesh['tm'=64,'state'=8] {'state'}, use_global_device_ids=true, to_apply=%region_32.33 | all-reduce | flops 1 | bytes 8 | tf_op jit(solution)/shard_map/pmax | solution.py:84
  874.1 13.3 %psum.7 = f32[]{:T(128)} all-reduce(f32[]{:T(128)} %exponential_reduce_fusion.2), channel_id=1, replica_groups=mesh['tm'=64,'state'=8] {'state'}, use_global_device_ids=true, to_apply=%region_34.35 | all-reduce | flops 1 | bytes 8 | tf_op jit(solution)/shard_map/psum | solution.py:85
  (244 shorter events, 268.6 us)
Async XLA Ops:
  6.5 6.5 copy-start.2
  6.5 6.3 copy-start.4
  6.5 6.5 copy-start.5
  6.5 41.3 %all-gather.6.cloned.1.call-start = ((), (), s32[]{:S(2)}) async-start(), calls=%async_computation | async-start | bytes 1769472 | tf_op jit(solution)/shard_map/all_gather | solution.py:44
  10.8 208.6 %all-gather.8.cloned.1.call-start = ((), (), s32[]{:S(2)}) async-start(), calls=%async_computation.1 | async-start | bytes 9437184 | tf_op jit(solution)/shard_map/all_gather | solution.py:60
  51.4 2.5 copy-start
  90.1 1.4 copy-start.1
  93.1 51.6 %collective-permute-start.1 = (f32[2048,256]{1,0:T(8,128)}, f32[2048,256]{1,0:T(8,128)S(1)}, u32[]{:S(2)}, u32[]{:S(2)}) collective-permute-start(f32[2048,256]{1,0:T(8,128)} %fusion.4), channel_id=1, source_target_pairs={{0,8},{8,16},{16,24},{24,32},{32,40},{40,48},{48,56},{56,64},{64,7... | collective-permute-start | bytes 6291464 | tf_op jit(solution)/shard_map/ppermute | solution.py:13
  157.9 1.4 copy-start.3
  228.7 7.4 collective-permute-start
  250.2 7.3 collective-permute-start
  269.5 7.3 collective-permute-start
  290.8 7.3 collective-permute-start
  310.1 7.3 collective-permute-start
  331.4 7.3 collective-permute-start
  350.7 7.3 collective-permute-start
  372.0 7.3 collective-permute-start
  391.4 7.3 collective-permute-start
  412.7 7.3 collective-permute-start
  432.0 7.3 collective-permute-start
  453.3 7.3 collective-permute-start
  472.6 7.3 collective-permute-start
  493.9 7.3 collective-permute-start
  513.2 7.3 collective-permute-start
  534.5 7.3 collective-permute-start
  553.9 7.3 collective-permute-start
  575.2 7.3 collective-permute-start
  594.5 7.3 collective-permute-start
  615.8 7.3 collective-permute-start
  635.1 7.3 collective-permute-start
  656.4 7.3 collective-permute-start
  675.7 7.3 collective-permute-start
  697.0 7.3 collective-permute-start
  716.4 7.3 collective-permute-start
  737.7 7.3 collective-permute-start
  757.0 7.3 collective-permute-start
  778.3 7.3 collective-permute-start
  797.6 7.3 collective-permute-start
  818.9 7.3 collective-permute-start
  838.2 7.3 collective-permute-start
Sparse Core Ops, SparseCore 0:
  10.9 36.9 all-gather.5
  159.4 59.8 all-gather.7
where the time goes:
time: 900 us; the launch traced here: 896 us
  blocking collectives  375 us (42%)
  waiting for transfers between devices  270 us (30%)
  other arithmetic  89.1 us (10%)
  starting transfers between devices  65.9 us (7%)
  matrix products  58.9 us (7%)
  local copies, waits for them, and re-layouts  21.8 us (2%)
  between operations  15 us (2%)
    all_gather x31, blocking collectives, advance(): whole_vector = lax.all_gather(incoming, 'state', axis=0, tiled=True)  309 us
    ppermute x32, waiting for transfers between devices, from_behind(): lax.ppermute(value, axis, [(source, source + steps) for source in range(i...  198 us
    ppermute x32, starting transfers between devices, from_behind(): lax.ppermute(value, axis, [(source, source + steps) for source in range(i...  65.9 us
    all_gather x1, waiting for transfers between devices, on_device(): lax.all_gather(weights, 'state', axis=1, tiled=True)  54.8 us
    dot_general x32, matrix products, apply_cols(): jnp.dot(jnp.exp(vector - vector_top)[None, :], scaled_exp, precision=lax....  29.6 us
    reduce_max x32, other arithmetic, apply_cols(): vector_top = jnp.max(vector)  22.9 us
    exp x32, other arithmetic, apply_cols(): jnp.exp(vector - vector_top)[None, :]  22.8 us
    select_n x31, other arithmetic, advance(): return jnp.where(position < 2, start_cols, apply_cols(whole_vector))  21.7 us
  transfers between devices with their start and end apart: 34, of which 34 were waited for; matrix products, arithmetic and copies ran while one was open for 1% of the time, Pallas kernels for 0%

commit v1 on v0

--- a/solution.py
+++ b/solution.py
@@ -1,3 +1,4 @@
+import functools
 import jax
 import jax.numpy as jnp
 from jax import lax
@@ -5,6 +6,35 @@
 
 SEQS = 1
 SMOOTH = 0.001
+
+
+def _name_tokens(a0, dim_at):
+    value_now = list(a0.shape[1:])
+    value_now[dim_at] *= a0.shape[0]
+    m_next = jnp.moveaxis(a0, 0, dim_at).reshape(value_now)
+    return m_next
+
+
+def desk_settle(field_in, dev_axis, axis_k):
+    axis_n = lax.axis_size(dev_axis)
+    crops = list(map(lambda jj: (jj, (jj + 1) % axis_n), range(axis_n)))
+    pages = [(i, p) for p, i in crops]
+    v1, spare = ([], [])
+    pp = 0
+    while pp < axis_n - 1:
+        if pp % 2 == 0:
+            v1.append(lax.ppermute(v1[-1] if v1 else field_in, dev_axis, crops))
+        else:
+            spare.append(lax.ppermute(spare[-1] if spare else field_in, dev_axis, pages))
+        pp += 1
+    ready = jnp.stack([*v1[::-1], field_in, *spare], axis=0)
+    r1 = lax.axis_index(dev_axis) - len(v1)
+    ready = ready[(jnp.arange(axis_n) - r1) % axis_n]
+    now = _name_tokens(ready, axis_k)
+    return now
+
+
+_place_hubs = functools.partial(desk_settle, dev_axis="state", axis_k=1)
 
 
 def from_behind(value, axis, steps):
@@ -56,11 +86,7 @@
     weights = jnp.exp(shifted - left_peak[:, None]).astype(jnp.bfloat16)
     right_exp = jnp.exp(own_log - row_peak[:, None]).astype(jnp.bfloat16)
     prior_log = jax.nn.log_softmax(init_logits)
-    summed = jnp.dot(
-        lax.all_gather(weights, "state", axis=1, tiled=True),
-        right_exp,
-        preferred_element_type=jnp.float32,
-    )
+    summed = jnp.dot(_place_hubs(weights), right_exp, preferred_element_type=jnp.float32)
     pair_log = left_peak[:, None] + jnp.log(summed)
     chosen = jnp.where(position == 0, own_log, pair_log)
     col_max = jnp.max(chosen, axis=0)

time: 900 us -> 938 us (1.042)
  the two profiles are of different devices: /device:TPU:9 before, /device:TPU:25 now
where the time goes in v1:
time: 938 us; the launch traced here: 934 us
  blocking collectives  382 us (41%)
  waiting for transfers between devices  249 us (27%)
  other arithmetic  92.9 us (10%)
  starting transfers between devices  80.9 us (9%)
  matrix products  57.7 us (6%)
  local copies, waits for them, and re-layouts  55 us (6%)
  between operations  15 us (2%)
    all_gather x31, blocking collectives, advance(): whole_vector = lax.all_gather(incoming, 'state', axis=0, tiled=True)  315 us
    ppermute x32, waiting for transfers between devices, from_behind(): lax.ppermute(value, axis, [(source, source + steps) for source in range(i...  201 us
    ppermute x32, starting transfers between devices, from_behind(): lax.ppermute(value, axis, [(source, source + steps) for source in range(i...  62.9 us
    ppermute x4, waiting for transfers between devices, desk_settle(): v1.append(lax.ppermute(v1[-1] if v1 else field_in, dev_axis, crops))  31.2 us
    dot_general x32, matrix products, apply_cols(): jnp.dot(jnp.exp(vector - vector_top)[None, :], scaled_exp, precision=lax....  29.6 us
    reduce_max x32, other arithmetic, apply_cols(): vector_top = jnp.max(vector)  22.9 us
    exp x32, other arithmetic, apply_cols(): jnp.exp(vector - vector_top)[None, :]  22.8 us
    select_n x31, other arithmetic, advance(): return jnp.where(position < 2, start_cols, apply_cols(whole_vector))  21.7 us
  transfers between devices with their start and end apart: 40, of which 37 were waited for; matrix products, arithmetic and copies ran while one was open for 3% of the time, Pallas kernels for 0%

profile of v1, /device:TPU:25, one launch (start us, length us, event | category | flops | bytes accessed | tf_op | source)
XLA Modules:
  0.0 934.3 jit_solution(10042890333654069536)
XLA Ops:
  13.2 13.6 %all_gather.12 = f32[8,2048]{1,0:T(8,128)S(1)} all-gather(f32[8,256]{1,0:T(8,128)S(1)} %fusion.15), channel_id=1, replica_groups=mesh['tm'=64,'state'=8] {'state'}, dimensions={1}, use_global_device_ids=true | all-gather | bytes 73728 | tf_op jit(solution)/shard_map/all_gather | solution.py:79
  30.5 17.2 %all-gather.5.cloned.1.call-done = bf16[16,3,128,128]{3,2,1,0:T(8,128)(2,1)} async-done(((bf16[2,3,128,128]{3,2,1,0:T(8,128)(2,1)}), bf16[16,3,128,128]{3,2,1,0:T(8,128)(2,1)}) %all-gather.5.cloned.1.call-update) | async-done | bytes 1572880 | tf_op jit(solution)/shard_map/all_gather | solution.py:74
  97.4 12.8 %pmax.21 = f32[2048]{0:T(1024)S(1)} all-reduce(f32[2048]{0:T(1024)S(1)} %bitcast.187), channel_id=1, replica_groups=mesh['tm'=64,'state'=8] {'state'}, use_global_device_ids=true, to_apply=%region_24.25 | all-reduce | flops 2048 | bytes 16384 | tf_op jit(solution)/shard_map/pmax | solution.py:82
  110.3 33.6 %collective-permute-done.1 = f32[2048,256]{1,0:T(8,128)S(1)} collective-permute-done((f32[2048,256]{1,0:T(8,128)}, f32[2048,256]{1,0:T(8,128)S(1)}, u32[]{:S(2)}, u32[]{:S(2)}) %collective-permute-start.1) | collective-permute-done | bytes 2097184 | tf_op jit(solution)/shard_map/ppermute | solution.py:43
  145.7 12.9 %pmax.22 = f32[2048]{0:T(1024)S(1)} all-reduce(f32[2048]{0:T(1024)S(1)} %add_reduce_fusion), channel_id=1, replica_groups=mesh['tm'=64,'state'=8] {'state'}, use_global_device_ids=true, to_apply=%region_26.27 | all-reduce | flops 2048 | bytes 16384 | tf_op jit(solution)/shard_map/pmax | solution.py:85
  161.5 12.1 %collective-permute-done.2 = bf16[2048,256]{1,0:T(8,128)(2,1)S(1)} collective-permute-done((bf16[2048,256]{1,0:T(8,128)(2,1)}, bf16[2048,256]{1,0:T(8,128)(2,1)S(1)}, u32[]{:S(2)}, u32[]{:S(2)}) %collective-permute-start.2) | collective-permute-done | bytes 1048608 | tf_op jit(solution)/shard_map/ppermute | solution.py:26
  179.1 9.5 %collective-permute-done.3 = bf16[2048,256]{1,0:T(8,128)(2,1)S(1)} collective-permute-done((bf16[2048,256]{1,0:T(8,128)(2,1)S(1)}, bf16[2048,256]{1,0:T(8,128)(2,1)S(1)}, u32[]{:S(2)}, u32[]{:S(2)}) %collective-permute-start.3) | collective-permute-done | bytes 1048608 | tf_op jit(solution)/shard_map/ppermute | solution.py:26
  195.4 7.5 collective-permute-done.4
  231.3 8.0 gather_fusion.8
  239.4 11.6 %copy.12 = bf16[2048,8,256]{0,2,1:T(8,128)(2,1)} copy(bf16[2048,8,256]{2,0,1:T(8,128)(2,1)} %bitcast.162) | data formatting | bytes 16777216 | tf_op jit(solution)/shard_map/transpose | solution.py:14
  250.9 6.3 fusion.23
  259.1 636.9 %while.12 = (s32[]{:T(128)}, f32[256]{0:T(256)S(1)}, pred[]{:T(512)}, f32[256]{0:T(256)S(1)}, f32[2048,256]{1,0:T(8,128)S(1)}, /*index=5*/f32[256]{0:T(256)S(1)}, s32[]{:T(128)}, f32[]{:T(128)}) while((s32[]{:T(128)}, f32[256]{0:T(256)S(1)}, pred[]{:T(512)}, f32[256]{0:T(256)S(1)}, f32[2048,256]{1,0:T(8,128)S(1)}, ...), condition=%wide.region_30.31_spmd, body=%wide.region_28.30_spmd.sunk | while | flops 6296321 | bytes 2148494 | solution.py:109
  261.0 5.4 collective-permute-done
  266.4 17.2 %all-gather.2 = f32[8,1,256]{2,1,0:T(1,128)S(1)} all-gather(f32[1,1,256]{2,1,0:T(1,128)S(1)} %bitcast.188), channel_id=1, replica_groups=mesh['tm'=64,'state'=8] {'state'}, dimensions={0}, use_global_device_ids=true | all-gather | bytes 9216 | tf_op jit(solution)/shard_map/while/body/eval_jaxpr/all_gather | solution.py:106
  288.5 5.4 collective-permute-done
  293.9 10.9 %all-gather.2 = f32[8,1,256]{2,1,0:T(1,128)S(1)} all-gather(f32[1,1,256]{2,1,0:T(1,128)S(1)} %bitcast.188), channel_id=1, replica_groups=mesh['tm'=64,'state'=8] {'state'}, dimensions={0}, use_global_device_ids=true | all-gather | bytes 9216 | tf_op jit(solution)/shard_map/while/body/eval_jaxpr/all_gather | solution.py:106
  309.8 5.4 collective-permute-done
  315.2 9.0 all-gather.2
  329.2 5.4 collective-permute-done
  334.6 10.9 %all-gather.2 = f32[8,1,256]{2,1,0:T(1,128)S(1)} all-gather(f32[1,1,256]{2,1,0:T(1,128)S(1)} %bitcast.188), channel_id=1, replica_groups=mesh['tm'=64,'state'=8] {'state'}, dimensions={0}, use_global_device_ids=true | all-gather | bytes 9216 | tf_op jit(solution)/shard_map/while/body/eval_jaxpr/all_gather | solution.py:106
  350.5 5.4 collective-permute-done
  355.8 9.0 all-gather.2
  369.8 5.4 collective-permute-done
  375.2 10.9 %all-gather.2 = f32[8,1,256]{2,1,0:T(1,128)S(1)} all-gather(f32[1,1,256]{2,1,0:T(1,128)S(1)} %bitcast.188), channel_id=1, replica_groups=mesh['tm'=64,'state'=8] {'state'}, dimensions={0}, use_global_device_ids=true | all-gather | bytes 9216 | tf_op jit(solution)/shard_map/while/body/eval_jaxpr/all_gather | solution.py:106
  396.5 9.0 all-gather.2
  415.8 10.9 %all-gather.2 = f32[8,1,256]{2,1,0:T(1,128)S(1)} all-gather(f32[1,1,256]{2,1,0:T(1,128)S(1)} %bitcast.188), channel_id=1, replica_groups=mesh['tm'=64,'state'=8] {'state'}, dimensions={0}, use_global_device_ids=true | all-gather | bytes 9216 | tf_op jit(solution)/shard_map/while/body/eval_jaxpr/all_gather | solution.py:106
  431.7 5.4 collective-permute-done
  437.1 9.0 all-gather.2
  451.0 5.4 collective-permute-done
  456.4 10.9 %all-gather.2 = f32[8,1,256]{2,1,0:T(1,128)S(1)} all-gather(f32[1,1,256]{2,1,0:T(1,128)S(1)} %bitcast.188), channel_id=1, replica_groups=mesh['tm'=64,'state'=8] {'state'}, dimensions={0}, use_global_device_ids=true | all-gather | bytes 9216 | tf_op jit(solution)/shard_map/while/body/eval_jaxpr/all_gather | solution.py:106
  472.3 5.4 collective-permute-done
  477.7 9.0 all-gather.2
  491.7 5.4 collective-permute-done
  497.1 10.9 %all-gather.2 = f32[8,1,256]{2,1,0:T(1,128)S(1)} all-gather(f32[1,1,256]{2,1,0:T(1,128)S(1)} %bitcast.188), channel_id=1, replica_groups=mesh['tm'=64,'state'=8] {'state'}, dimensions={0}, use_global_device_ids=true | all-gather | bytes 9216 | tf_op jit(solution)/shard_map/while/body/eval_jaxpr/all_gather | solution.py:106
  513.0 5.4 collective-permute-done
  518.3 9.0 all-gather.2
  532.3 5.4 collective-permute-done
  537.7 10.9 %all-gather.2 = f32[8,1,256]{2,1,0:T(1,128)S(1)} all-gather(f32[1,1,256]{2,1,0:T(1,128)S(1)} %bitcast.188), channel_id=1, replica_groups=mesh['tm'=64,'state'=8] {'state'}, dimensions={0}, use_global_device_ids=true | all-gather | bytes 9216 | tf_op jit(solution)/shard_map/while/body/eval_jaxpr/all_gather | solution.py:106
  553.6 5.4 collective-permute-done
  559.0 9.0 all-gather.2
  572.9 5.4 collective-permute-done
  578.3 10.9 %all-gather.2 = f32[8,1,256]{2,1,0:T(1,128)S(1)} all-gather(f32[1,1,256]{2,1,0:T(1,128)S(1)} %bitcast.188), channel_id=1, replica_groups=mesh['tm'=64,'state'=8] {'state'}, dimensions={0}, use_global_device_ids=true | all-gather | bytes 9216 | tf_op jit(solution)/shard_map/while/body/eval_jaxpr/all_gather | solution.py:106
  594.2 5.4 collective-permute-done
  599.6 9.0 all-gather.2
  613.5 5.4 collective-permute-done
  618.9 10.9 %all-gather.2 = f32[8,1,256]{2,1,0:T(1,128)S(1)} all-gather(f32[1,1,256]{2,1,0:T(1,128)S(1)} %bitcast.188), channel_id=1, replica_groups=mesh['tm'=64,'state'=8] {'state'}, dimensions={0}, use_global_device_ids=true | all-gather | bytes 9216 | tf_op jit(solution)/shard_map/while/body/eval_jaxpr/all_gather | solution.py:106
  640.2 9.0 all-gather.2
  659.6 10.9 %all-gather.2 = f32[8,1,256]{2,1,0:T(1,128)S(1)} all-gather(f32[1,1,256]{2,1,0:T(1,128)S(1)} %bitcast.188), channel_id=1, replica_groups=mesh['tm'=64,'state'=8] {'state'}, dimensions={0}, use_global_device_ids=true | all-gather | bytes 9216 | tf_op jit(solution)/shard_map/while/body/eval_jaxpr/all_gather | solution.py:106
  675.4 5.4 collective-permute-done
  680.8 9.0 all-gather.2
  694.8 5.4 collective-permute-done
  700.2 10.9 %all-gather.2 = f32[8,1,256]{2,1,0:T(1,128)S(1)} all-gather(f32[1,1,256]{2,1,0:T(1,128)S(1)} %bitcast.188), channel_id=1, replica_groups=mesh['tm'=64,'state'=8] {'state'}, dimensions={0}, use_global_device_ids=true | all-gather | bytes 9216 | tf_op jit(solution)/shard_map/while/body/eval_jaxpr/all_gather | solution.py:106
  716.1 5.4 collective-permute-done
  721.5 9.0 all-gather.2
  740.8 10.9 %all-gather.2 = f32[8,1,256]{2,1,0:T(1,128)S(1)} all-gather(f32[1,1,256]{2,1,0:T(1,128)S(1)} %bitcast.188), channel_id=1, replica_groups=mesh['tm'=64,'state'=8] {'state'}, dimensions={0}, use_global_device_ids=true | all-gather | bytes 9216 | tf_op jit(solution)/shard_map/while/body/eval_jaxpr/all_gather | solution.py:106
  762.1 9.0 all-gather.2
  781.4 10.9 %all-gather.2 = f32[8,1,256]{2,1,0:T(1,128)S(1)} all-gather(f32[1,1,256]{2,1,0:T(1,128)S(1)} %bitcast.188), channel_id=1, replica_groups=mesh['tm'=64,'state'=8] {'state'}, dimensions={0}, use_global_device_ids=true | all-gather | bytes 9216 | tf_op jit(solution)/shard_map/while/body/eval_jaxpr/all_gather | solution.py:106
  802.7 9.0 all-gather.2
  822.1 10.9 %all-gather.2 = f32[8,1,256]{2,1,0:T(1,128)S(1)} all-gather(f32[1,1,256]{2,1,0:T(1,128)S(1)} %bitcast.188), channel_id=1, replica_groups=mesh['tm'=64,'state'=8] {'state'}, dimensions={0}, use_global_device_ids=true | all-gather | bytes 9216 | tf_op jit(solution)/shard_map/while/body/eval_jaxpr/all_gather | solution.py:106
  843.3 9.0 all-gather.2
  862.7 10.9 %all-gather.2 = f32[8,1,256]{2,1,0:T(1,128)S(1)} all-gather(f32[1,1,256]{2,1,0:T(1,128)S(1)} %bitcast.188), channel_id=1, replica_groups=mesh['tm'=64,'state'=8] {'state'}, dimensions={0}, use_global_device_ids=true | all-gather | bytes 9216 | tf_op jit(solution)/shard_map/while/body/eval_jaxpr/all_gather | solution.py:106
  884.0 9.0 all-gather.2
  896.6 12.7 %pmax.23 = f32[]{:T(128)} all-reduce(f32[]{:T(128)} %reduce_max.175), channel_id=1, replica_groups=mesh['tm'=64,'state'=8] {'state'}, use_global_device_ids=true, to_apply=%region_32.33 | all-reduce | flops 1 | bytes 8 | tf_op jit(solution)/shard_map/pmax | solution.py:110
  910.5 14.9 %psum.7 = f32[]{:T(128)} all-reduce(f32[]{:T(128)} %exponential_reduce_fusion.2), channel_id=1, replica_groups=mesh['tm'=64,'state'=8] {'state'}, use_global_device_ids=true, to_apply=%region_34.35 | all-reduce | flops 1 | bytes 8 | tf_op jit(solution)/shard_map/psum | solution.py:111
  (282 shorter events, 327.5 us)
Async XLA Ops:
  6.5 6.5 copy-start.5
  6.5 6.3 copy-start.11
  6.5 6.5 copy-start.12
  6.5 41.2 %all-gather.5.cloned.1.call-start = ((), (), s32[]{:S(2)}) async-start(), calls=%async_computation | async-start | bytes 1769472 | tf_op jit(solution)/shard_map/all_gather | solution.py:74
  51.2 2.5 copy-start
  89.8 2.1 copy-start.1
  91.9 52.0 %collective-permute-start.1 = (f32[2048,256]{1,0:T(8,128)}, f32[2048,256]{1,0:T(8,128)S(1)}, u32[]{:S(2)}, u32[]{:S(2)}) collective-permute-start(f32[2048,256]{1,0:T(8,128)} %fusion.4), channel_id=1, source_target_pairs={{0,8},{8,16},{16,24},{24,32},{32,40},{40,48},{48,56},{56,64},{64,7... | collective-permute-start | bytes 6291464 | tf_op jit(solution)/shard_map/ppermute | solution.py:43
  143.9 1.4 copy-start.3
  145.6 45.5 %copy-start.10 = (f32[2048]{0:T(1024)S(1)}, f32[2048]{0:T(1024)}, u32[]{:S(2)}) copy-start(f32[2048]{0:T(1024)} %param.11) | copy-start | bytes 24580
  145.6 64.3 %copy-start.2 = (f32[16,128,256,1]{2,1,3,0:T(8,128)S(1)}, f32[16,128,256,1]{2,1,3,0:T(8,128)}, u32[]{:S(2)}) copy-start(f32[16,128,256,1]{2,1,3,0:T(8,128)} %copy-done.1) | copy-start | bytes 6291460
  161.5 12.1 %collective-permute-start.2 = (bf16[2048,256]{1,0:T(8,128)(2,1)}, bf16[2048,256]{1,0:T(8,128)(2,1)S(1)}, u32[]{:S(2)}, u32[]{:S(2)}) collective-permute-start(bf16[2048,256]{1,0:T(8,128)(2,1)} %exponential_convert_fusion.1), channel_id=1, source_target_pairs={{0,1},{1,2},{2,3},{3,4},{4,5},{5,6},{6,7},{7,0},{8,9},{9,10},{10,1... | collective-permute-start | bytes 3145736 | tf_op jit(solution)/shard_map/ppermute | solution.py:26
  173.5 1.0 copy-start.6
  174.5 14.1 %collective-permute-start.3 = (bf16[2048,256]{1,0:T(8,128)(2,1)S(1)}, bf16[2048,256]{1,0:T(8,128)(2,1)S(1)}, u32[]{:S(2)}, u32[]{:S(2)}) collective-permute-start(bf16[2048,256]{1,0:T(8,128)(2,1)S(1)} %collective-permute-done.2), channel_id=1, source_target_pairs={{0,1},{1,2},{2,3},{3,4},{4,5},{5,6},{6,7},{7,0},{8,9},{9,10},{10,1... | collective-permute-start | bytes 3145736 | tf_op jit(solution)/shard_map/ppermute | solution.py:26
  176.9 14.9 %collective-permute-start.6 = (bf16[2048,256]{1,0:T(8,128)(2,1)}, bf16[2048,256]{1,0:T(8,128)(2,1)}, u32[]{:S(2)}, u32[]{:S(2)}) collective-permute-start(bf16[2048,256]{1,0:T(8,128)(2,1)} %exponential_convert_fusion.1), channel_id=1, source_target_pairs={{1,0},{2,1},{3,2},{4,3},{5,4},{6,5},{7,6},{0,7},{9,8},{10,9},{11,1... | collective-permute-start | bytes 3145736 | tf_op jit(solution)/shard_map/ppermute | solution.py:28
  188.6 21.4 %copy-start.8 = (bf16[2048,256]{1,0:T(8,128)(2,1)}, bf16[2048,256]{1,0:T(8,128)(2,1)S(1)}, u32[]{:S(2)}) copy-start(bf16[2048,256]{1,0:T(8,128)(2,1)S(1)} %collective-permute-done.3) | copy-start | bytes 3145732
  188.6 14.2 %collective-permute-start.4 = (bf16[2048,256]{1,0:T(8,128)(2,1)S(1)}, bf16[2048,256]{1,0:T(8,128)(2,1)}, u32[]{:S(2)}, u32[]{:S(2)}) collective-permute-start(bf16[2048,256]{1,0:T(8,128)(2,1)S(1)} %collective-permute-done.3), channel_id=1, source_target_pairs={{0,1},{1,2},{2,3},{3,4},{4,5},{5,6},{6,7},{7,0},{8,9},{9,10},{10,1... | collective-permute-start | bytes 3145736 | tf_op jit(solution)/shard_map/ppermute | solution.py:26
  191.8 18.8 %collective-permute-start.7 = (bf16[2048,256]{1,0:T(8,128)(2,1)}, bf16[2048,256]{1,0:T(8,128)(2,1)}, u32[]{:S(2)}, u32[]{:S(2)}) collective-permute-start(bf16[2048,256]{1,0:T(8,128)(2,1)} %collective-permute-done.6), channel_id=1, source_target_pairs={{1,0},{2,1},{3,2},{4,3},{5,4},{6,5},{7,6},{0,7},{9,8},{10,9},{11,1... | collective-permute-start | bytes 3145736 | tf_op jit(solution)/shard_map/ppermute | solution.py:28
  202.8 14.6 %collective-permute-start.5 = (bf16[2048,256]{1,0:T(8,128)(2,1)}, bf16[2048,256]{1,0:T(8,128)(2,1)}, u32[]{:S(2)}, u32[]{:S(2)}) collective-permute-start(bf16[2048,256]{1,0:T(8,128)(2,1)} %collective-permute-done.4), channel_id=1, source_target_pairs={{0,1},{1,2},{2,3},{3,4},{4,5},{5,6},{6,7},{7,0},{8,9},{9,10},{10,1... | collective-permute-start | bytes 3145736 | tf_op jit(solution)/shard_map/ppermute | solution.py:26
  210.6 11.6 %copy-start.9 = (bf16[2048,256]{1,0:T(8,128)(2,1)S(1)}, bf16[2048,256]{1,0:T(8,128)(2,1)}, u32[]{:S(2)}) copy-start(bf16[2048,256]{1,0:T(8,128)(2,1)} %copy-done.8) | copy-start | bytes 3145732
  210.6 19.6 %collective-permute-start.8 = (bf16[2048,256]{1,0:T(8,128)(2,1)}, bf16[2048,256]{1,0:T(8,128)(2,1)S(1)}, u32[]{:S(2)}, u32[]{:S(2)}) collective-permute-start(bf16[2048,256]{1,0:T(8,128)(2,1)} %collective-permute-done.7), channel_id=1, source_target_pairs={{1,0},{2,1},{3,2},{4,3},{5,4},{6,5},{7,6},{0,7},{9,8},{10,9},{11,1... | collective-permute-start | bytes 3145736 | tf_op jit(solution)/shard_map/ppermute | solution.py:28
  219.8 3.5 copy-start.7
  222.2 2.1 copy-start.4
  259.1 7.3 collective-permute-start
  286.6 7.3 collective-permute-start
  307.9 7.3 collective-permute-start
  327.2 7.3 collective-permute-start
  348.5 7.3 collective-permute-start
  367.9 7.3 collective-permute-start
  389.1 7.3 collective-permute-start
  408.5 7.3 collective-permute-start
  429.8 7.3 collective-permute-start
  449.1 7.3 collective-permute-start
  470.4 7.3 collective-permute-start
  489.7 7.3 collective-permute-start
  511.0 7.3 collective-permute-start
  530.4 7.3 collective-permute-start
  551.6 7.3 collective-permute-start
  571.0 7.3 collective-permute-start
  592.3 7.3 collective-permute-start
  611.6 7.3 collective-permute-start
  632.9 7.3 collective-permute-start
  652.2 7.3 collective-permute-start
  673.5 7.3 collective-permute-start
  692.9 7.3 collective-permute-start
  714.1 7.3 collective-permute-start
  733.5 7.3 collective-permute-start
  754.8 7.3 collective-permute-start
  774.1 7.3 collective-permute-start
  795.4 7.3 collective-permute-start
  814.7 7.3 collective-permute-start
  836.0 7.3 collective-permute-start
  855.4 7.3 collective-permute-start
  876.6 7.3 collective-permute-start
Sparse Core Ops, SparseCore 0:
  10.9 36.7 all-gather.4
